TPU v7x, 512 devices: a whole 4x4x16 slice. The times are simulated.
512 devices in a mesh: dp: 128 (over y, z, core), mp: 4 (over x).
Axes of the slice: x: 4, y: 4, z: 16, core: 2. Of those that a mesh axis runs over, the one named last changes fastest.
Arguments:
- embeddings: bfloat16 [32768, 768], P('dp'), may hold values from -8192 to 8192
- cluster_ids: int32 [32768], P('dp'), may hold values from 0 to 511, as said below
Outputs:
- scores: float32 [32768], P('dp')
Inputs may be any that keep to these rules, and one draw needn't show every extreme that they name: `cluster_ids`: the owner of cluster c is the index c // 4 of dp. Of the 256 rows of one index of dp, at most 4 lie in the clusters of one owner, and some owner gets exactly 4 rows from every index of dp.
All inputs are finite; a program needn't handle non-finite values.
Results may differ from a plain program's by a relative error of at most 0.0018.
Values may be sent and summed in bfloat16 or wider, within the bound.
A program may use at most 64 MiB of HBM per device.

v0:
```python
import jax
import jax.numpy as jnp
from jax import lax
from jax.sharding import PartitionSpec as P

CPO = 4


def contract_rows(left_rows, right_rows):
    return lax.dot_general(
        left_rows, right_rows, (((0,), (0,)), ((), ())), preferred_element_type=jnp.float32
    )


def normalize_rows(values):
    widened = values.astype(jnp.float32)
    square_sum = jnp.sum(widened * widened, axis=1, keepdims=True)
    inverse_norm = lax.rsqrt(square_sum + 1e-06)
    return (widened * inverse_norm).astype(jnp.bfloat16)


def best_match(queries, query_ids, query_start, key_units, key_ids):
    similarity = lax.dot_general(
        queries, key_units, (((1,), (1,)), ((), ())), preferred_element_type=jnp.float32
    )
    query_pos = query_start + jnp.arange(queries.shape[0], dtype=jnp.int32)
    key_pos = jnp.arange(key_units.shape[0], dtype=jnp.int32)
    same_cluster = (
        (query_ids[:, None] == key_ids[None, :])
        & (query_ids[:, None] >= 0)
        & (query_pos[:, None] != key_pos[None, :])
    )
    return jnp.max(jnp.where(same_cluster, similarity, -1.0), axis=1)


def local(embeddings, cluster_ids):
    row_count, feat_width = embeddings.shape
    dp_count = lax.axis_size("dp")
    mp_count = lax.axis_size("mp")
    mp_index = lax.axis_index("mp")
    pair_cap = 2 * row_count // dp_count
    slot_count = dp_count * pair_cap
    quarter_len = slot_count // mp_count
    identity = jnp.eye(feat_width, dtype=jnp.float32)
    row_share = row_count // mp_count
    own_rows = lax.dynamic_slice_in_dim(embeddings, mp_index * row_share, row_share, 0)
    moments = lax.psum(contract_rows(own_rows, own_rows), ("dp", "mp"))
    chol_factor = jnp.linalg.cholesky(moments / float(row_count * dp_count) + 0.001 * identity)
    whitening = jax.scipy.linalg.solve_triangular(chol_factor, identity, lower=True).astype(
        jnp.bfloat16
    )
    owner_ids = cluster_ids // CPO
    owner_hits = (owner_ids[:, None] == jnp.arange(dp_count, dtype=jnp.int32)[None, :]).astype(
        jnp.int32
    )
    earlier_hits = jnp.cumsum(owner_hits, axis=0) - owner_hits
    row_rank = jnp.sum(earlier_hits * owner_hits, axis=1)
    col_share = feat_width // mp_count
    whiten_part = lax.dynamic_slice_in_dim(whitening, mp_index * col_share, col_share, 0)
    whitened = lax.dot_general(
        embeddings, whiten_part, (((1,), (1,)), ((), ())), preferred_element_type=jnp.float32
    ).astype(jnp.bfloat16)
    slot_index = owner_ids * pair_cap + row_rank
    send_rows = jnp.zeros((slot_count, col_share), jnp.bfloat16).at[slot_index].set(whitened)
    send_ids = jnp.full((slot_count,), -1, jnp.int32).at[slot_index].set(cluster_ids)
    got_rows, got_ids = (
        lax.all_to_all(send_rows, "dp", split_axis=0, concat_axis=0, tiled=True),
        lax.all_to_all(send_ids, "dp", split_axis=0, concat_axis=0, tiled=True),
    )
    key_rows = lax.all_gather(got_rows, "mp", axis=1, tiled=True)
    unit = normalize_rows(key_rows)
    query_start = mp_index * quarter_len
    queries = lax.dynamic_slice_in_dim(unit, query_start, quarter_len, 0)
    query_ids = lax.dynamic_slice_in_dim(got_ids, query_start, quarter_len, 0)
    best_score = best_match(queries, query_ids, query_start, unit, got_ids)
    all_scores = lax.all_gather(best_score, "mp", axis=0, tiled=True)
    returned = lax.all_to_all(all_scores, "dp", split_axis=0, concat_axis=0, tiled=True)
    return returned[slot_index]


def solution(mesh):
    in_specs = (P("dp", None), P("dp"))
    out_specs = P("dp")
    return jax.shard_map(local, mesh=mesh, in_specs=in_specs, out_specs=out_specs, check_vma=False)
```

profile of v0, /device:TPU:1, one launch (start us, length us, event | category | flops | bytes accessed | tf_op | source)
XLA Modules:
  0.0 857.0 jit_solution(18049372178460269238)
XLA Ops:
  7.5 2.0 fusion.53
  10.2 1.4 scatter_custom_fusion
  12.3 20.5 %all-to-all-start = ((s32[128,4,1]{1,2,0:T(1,128)}), s32[128,4,1]{1,2,0:T(1,128)S(1)}, u32[]{:S(2)}, u32[]{:S(2)}) async-start(s32[128,4,1]{1,2,0:T(1,128)} %bitcast.4), calls=%async_computation | async-start | bytes 131072 | tf_op jit(solution)/shard_map/all_to_all | solution.py:68
  33.9 1.6 fusion.11
  35.4 467.5 %all-reduce.3.cloned.1.call-done = f32[768,768]{0,1:T(8,128)} async-done(((f32[768,768]{0,1:T(8,128)}), f32[768,768]{0,1:T(8,128)}) %all-reduce.3.cloned.1.call-update) | async-done | bytes 2359312 | tf_op jit(solution)/shard_map/psum | solution.py:47
  502.9 3.3 select_add_fusion
  506.3 3.7 copy.39
  510.0 2.0 fusion
  512.0 1.4 copy-done.3
  513.3 11.7 %cholesky.164 = f32[128,128]{1,0:T(8,128)S(1)} custom-call(f32[128,128]{1,0:T(8,128)S(1)} %cholesky.421), custom_call_target="Cholesky" | custom-call | tf_op jit(solution)/shard_map/jit(cholesky)/cholesky | solution.py:48
  525.1 9.8 %custom-call.47 = f32[1,128,128]{1,2,0:T(8,128)S(1)} custom-call(f32[1,128,128]{2,1,0:T(8,128)S(1)} %get-tuple-element.46), custom_call_target="InvertDiagBlocksLowerTriangular" | custom-call | tf_op jit(solution)/shard_map/jit(cholesky)/cholesky | solution.py:48
  534.9 1.4 fusion.33
  536.3 1.4 convolution_subtract_fusion.4
  537.7 11.7 %cholesky.187 = f32[128,128]{1,0:T(8,128)S(1)} custom-call(f32[128,128]{1,0:T(8,128)S(1)} %cholesky.425), custom_call_target="Cholesky" | custom-call | tf_op jit(solution)/shard_map/jit(cholesky)/cholesky | solution.py:48
  550.5 10.6 %custom-call.48 = f32[1,128,128]{1,2,0:T(8,128)} custom-call(f32[1,128,128]{2,1,0:T(8,128)S(1)} %get-tuple-element.44), custom_call_target="InvertDiagBlocksLowerTriangular" | custom-call | tf_op jit(solution)/shard_map/jit(cholesky)/cholesky | solution.py:48
  562.5 1.9 convolution_subtract_fusion.5
  564.5 11.7 %cholesky.352 = f32[128,128]{1,0:T(8,128)S(1)} custom-call(f32[128,128]{1,0:T(8,128)S(1)} %cholesky.430), custom_call_target="Cholesky" | custom-call | tf_op jit(solution)/shard_map/jit(cholesky)/cholesky | solution.py:48
  576.4 9.8 %custom-call.49 = f32[1,128,128]{1,2,0:T(8,128)S(1)} custom-call(f32[1,128,128]{2,1,0:T(8,128)S(1)} %get-tuple-element.42), custom_call_target="InvertDiagBlocksLowerTriangular" | custom-call | tf_op jit(solution)/shard_map/jit(cholesky)/cholesky | solution.py:48
  586.6 2.1 convolution_subtract_fusion.6
  588.7 12.1 %cholesky.371 = f32[128,128]{1,0:T(8,128)S(1)} custom-call(f32[128,128]{1,0:T(8,128)S(1)} %cholesky.435), custom_call_target="Cholesky" | custom-call | tf_op jit(solution)/shard_map/jit(cholesky)/cholesky | solution.py:48
  600.9 9.8 %custom-call.50 = f32[1,128,128]{1,2,0:T(8,128)S(1)} custom-call(f32[1,128,128]{2,1,0:T(8,128)S(1)} %get-tuple-element.40), custom_call_target="InvertDiagBlocksLowerTriangular" | custom-call | tf_op jit(solution)/shard_map/jit(cholesky)/cholesky | solution.py:48
  611.1 1.9 convolution_subtract_fusion.7
  613.0 11.7 %cholesky.390 = f32[128,128]{1,0:T(8,128)S(1)} custom-call(f32[128,128]{1,0:T(8,128)S(1)} %cholesky.440), custom_call_target="Cholesky" | custom-call | tf_op jit(solution)/shard_map/jit(cholesky)/cholesky | solution.py:48
  624.8 9.8 %custom-call.51 = f32[1,128,128]{1,2,0:T(8,128)S(1)} custom-call(f32[1,128,128]{2,1,0:T(8,128)S(1)} %get-tuple-element.38), custom_call_target="InvertDiagBlocksLowerTriangular" | custom-call | tf_op jit(solution)/shard_map/jit(cholesky)/cholesky | solution.py:48
  634.9 1.7 convolution_subtract_fusion.8
  636.7 11.7 %cholesky.408 = f32[128,128]{1,0:T(8,128)S(1)} custom-call(f32[128,128]{1,0:T(8,128)S(1)} %convolution_subtract_fusion.8), custom_call_target="Cholesky" | custom-call | tf_op jit(solution)/shard_map/jit(cholesky)/cholesky | solution.py:48
  655.5 1.6 select_select_fusion
  657.1 21.3 %while.1 = (s32[]{:T(128)}, f32[768,768]{0,1:T(8,128)}, s32[6,2]{0,1:T(2,128)S(1)}, f32[6,128,128]{2,1,0:T(8,128)}, s32[]{:T(128)}) while((s32[]{:T(128)}, f32[768,768]{0,1:T(8,128)}, s32[6,2]{0,1:T(2,128)S(1)}, f32[6,128,128]{2,1,0:T(8,128)}, s32[]{:T(128)}) %tuple.34), condition=%wide.while_cond, body=%wide.while_body.sunk | while | flops 2 | bytes 393829 | solution.py:49
  657.7 2.2 dynamic-slice.7
  661.3 2.2 dynamic-slice.7
  664.9 2.2 dynamic-slice.7
  668.4 2.2 dynamic-slice.7
  672.0 2.2 dynamic-slice.7
  675.5 2.1 dynamic-slice.7
  678.4 59.9 %custom-call.52 = f32[6,128,128]{1,2,0:T(8,128)S(1)} custom-call(f32[6,128,128]{2,1,0:T(8,128)} %get-tuple-element.12), custom_call_target="InvertDiagBlocksLowerTriangular" | custom-call | tf_op jit(solution)/shard_map/jit(_solve_triangular)/triangular_solve | solution.py:49
  739.5 1.8 convolution_subtract_fusion.2
  741.9 2.3 convolution_subtract_fusion.3
  744.8 3.0 convolution_subtract_fusion.1
  748.4 3.6 fusion.12
  752.6 4.6 convolution_subtract_fusion
  758.2 1.5 scatter_custom_fusion.1
  760.5 15.3 %all-to-all-start.1 = ((bf16[128,4,192]{2,1,0:T(4,128)(2,1)}), bf16[128,4,192]{2,1,0:T(4,128)(2,1)S(1)}, u32[]{:S(2)}, u32[]{:S(2)}) async-start(bf16[128,4,192]{2,1,0:T(4,128)(2,1)} %all_to_all.27), calls=%async_computation.1 | async-start | bytes 524288 | tf_op jit(solution)/shard_map/all_to_all | solution.py:67
  777.3 20.9 %all-to-all-done.1 = bf16[128,4,192]{2,1,0:T(4,128)(2,1)S(1)} async-done(((bf16[128,4,192]{2,1,0:T(4,128)(2,1)}), bf16[128,4,192]{2,1,0:T(4,128)(2,1)S(1)}, u32[]{:S(2)}, u32[]{:S(2)}) %all-to-all-start.1) | async-done | bytes 196640 | tf_op jit(solution)/shard_map/all_to_all | solution.py:67
  798.5 11.0 %all_gather.6 = bf16[512,768]{0,1:T(8,128)(2,1)S(1)} all-gather(bf16[512,192]{0,1:T(8,128)(2,1)S(1)} %copy.58), channel_id=1, replica_groups=mesh['dp'=128,'mp'=4] {'mp'}, dimensions={1}, use_global_device_ids=true | all-gather | bytes 983040 | tf_op jit(solution)/shard_map/all_gather | solution.py:70
  810.2 8.2 all-gather
  820.3 11.1 %all-to-all-start.2 = ((f32[128,4,1]{1,2,0:T(1,128)}), f32[128,4,1]{1,2,0:T(1,128)S(1)}, u32[]{:S(2)}, u32[]{:S(2)}) async-start(f32[128,4,1]{1,2,0:T(1,128)} %bitcast.24), calls=%async_computation.2 | async-start | bytes 131072 | tf_op jit(solution)/shard_map/all_to_all | solution.py:77
  831.4 15.1 %all-to-all-done.2 = f32[128,4,1]{1,2,0:T(1,128)S(1)} async-done(((f32[128,4,1]{1,2,0:T(1,128)}), f32[128,4,1]{1,2,0:T(1,128)S(1)}, u32[]{:S(2)}, u32[]{:S(2)}) %all-to-all-start.2) | async-done | bytes 2080 | tf_op jit(solution)/shard_map/all_to_all | solution.py:77
  847.4 2.5 gather_fusion
  (120 shorter events, 29.5 us)
Async XLA Ops:
  6.5 1.0 copy-start
  6.5 496.4 %all-reduce.3.cloned.1.call-start = ((), (), s32[]{:S(2)}) async-start(), calls=%async_computation.3 | async-start | bytes 4718592 | tf_op jit(solution)/shard_map/psum | solution.py:47
  7.5 2.0 copy-start.5
  12.3 748.2 %all-to-all-start = ((s32[128,4,1]{1,2,0:T(1,128)}), s32[128,4,1]{1,2,0:T(1,128)S(1)}, u32[]{:S(2)}, u32[]{:S(2)}) async-start(s32[128,4,1]{1,2,0:T(1,128)} %bitcast.4), calls=%async_computation | async-start | bytes 131072 | tf_op jit(solution)/shard_map/all_to_all | solution.py:68
  506.3 3.7 copy-start.1
  511.9 1.4 copy-start.3
  561.0 1.1 copy-start.4
  678.4 63.5 %copy-start.2 = (f32[768,768]{0,1:T(8,128)S(1)}, f32[768,768]{0,1:T(8,128)}, u32[]{:S(2)}) copy-start(f32[768,768]{0,1:T(8,128)} %fusion.11) | copy-start | bytes 7077892
  760.5 37.7 %all-to-all-start.1 = ((bf16[128,4,192]{2,1,0:T(4,128)(2,1)}), bf16[128,4,192]{2,1,0:T(4,128)(2,1)S(1)}, u32[]{:S(2)}, u32[]{:S(2)}) async-start(bf16[128,4,192]{2,1,0:T(4,128)(2,1)} %all_to_all.27), calls=%async_computation.1 | async-start | bytes 524288 | tf_op jit(solution)/shard_map/all_to_all | solution.py:67
  820.3 26.2 %all-to-all-start.2 = ((f32[128,4,1]{1,2,0:T(1,128)}), f32[128,4,1]{1,2,0:T(1,128)S(1)}, u32[]{:S(2)}, u32[]{:S(2)}) async-start(f32[128,4,1]{1,2,0:T(1,128)} %bitcast.24), calls=%async_computation.2 | async-start | bytes 131072 | tf_op jit(solution)/shard_map/all_to_all | solution.py:77
Sparse Core Ops, SparseCore 0:
  12.6 490.2 all-reduce.2
where the time goes:
time: 862 us; the launch traced here: 857 us
  waiting for transfers between devices  503 us (58%)
  other arithmetic  197 us (23%)
  starting transfers between devices  47 us (5%)
  local copies, waits for them, and re-layouts  39.3 us (5%)
  matrix products  33.7 us (4%)
  blocking collectives  19.1 us (2%)
  between operations  17.9 us (2%)
    psum x1, waiting for transfers between devices, local(): moments = lax.psum(contract_rows(own_rows, own_rows), ('dp', 'mp'))  468 us
    another operation x22, other arithmetic, local(): jnp.linalg.cholesky(moments / float(row_count * dp_count) + 0.001 * ident...  124 us
    another operation x3, other arithmetic, local(): jax.scipy.linalg.solve_triangular(chol_factor, identity, lower=True)  61.5 us
    another operation x33, local copies, waits for them, and re-layouts  21.2 us
    all_to_all x1, waiting for transfers between devices, local(): lax.all_to_all(send_rows, 'dp', split_axis=0, concat_axis=0, tiled=True)  20.9 us
    all_to_all x1, starting transfers between devices, local(): lax.all_to_all(send_ids, 'dp', split_axis=0, concat_axis=0, tiled=True)  20.5 us
    another operation x11, matrix products, local(): jax.scipy.linalg.solve_triangular(chol_factor, identity, lower=True)  19.2 us
  transfers between devices with their start and end apart: 4, of which 3 were waited for; matrix products, arithmetic and copies ran while one was open for 30% of the time, Pallas kernels for 0%

commit v1 on v0

--- a/solution.py
+++ b/solution.py
@@ -44,7 +44,7 @@
     identity = jnp.eye(feat_width, dtype=jnp.float32)
     row_share = row_count // mp_count
     own_rows = lax.dynamic_slice_in_dim(embeddings, mp_index * row_share, row_share, 0)
-    moments = lax.psum(contract_rows(own_rows, own_rows), ("dp", "mp"))
+    moments = lax.psum(lax.psum(contract_rows(own_rows, own_rows), "dp"), "mp")
     chol_factor = jnp.linalg.cholesky(moments / float(row_count * dp_count) + 0.001 * identity)
     whitening = jax.scipy.linalg.solve_triangular(chol_factor, identity, lower=True).astype(
         jnp.bfloat16

time: 862 us -> 807 us (0.936)
  waiting for transfers between devices: 503 us -> 455 us
    psum x1 -> x2, waiting for transfers between devices: 468 us -> 419 us  [local(): moments = lax.psum(lax.psum(contract_rows(own_rows, own_rows), 'dp'), 'mp')]
  transfers between devices with their start and end apart: 4 -> 5, of which waited for: 3 -> 4; matrix products, arithmetic and copies ran while one was open for 30% -> 32% of each run, Pallas kernels for 0% -> 0%
where the time goes in v1:
time: 807 us; the launch traced here: 802 us
  waiting for transfers between devices  455 us (56%)
  other arithmetic  197 us (24%)
  starting transfers between devices  42.8 us (5%)
  local copies, waits for them, and re-layouts  39.3 us (5%)
  matrix products  33.6 us (4%)
  between operations  17.9 us (2%)
  blocking collectives  16.9 us (2%)
    psum x2, waiting for transfers between devices, local(): moments = lax.psum(lax.psum(contract_rows(own_rows, own_rows), 'dp'), 'mp')  419 us
    another operation x22, other arithmetic, local(): jnp.linalg.cholesky(moments / float(row_count * dp_count) + 0.001 * ident...  124 us
    another operation x3, other arithmetic, local(): jax.scipy.linalg.solve_triangular(chol_factor, identity, lower=True)  61.5 us
    another operation x33, local copies, waits for them, and re-layouts  21.2 us
    all_to_all x1, waiting for transfers between devices, local(): lax.all_to_all(send_rows, 'dp', split_axis=0, concat_axis=0, tiled=True)  20.9 us
    another operation x11, matrix products, local(): jax.scipy.linalg.solve_triangular(chol_factor, identity, lower=True)  19.2 us
    all_to_all x1, starting transfers between devices, local(): lax.all_to_all(send_rows, 'dp', split_axis=0, concat_axis=0, tiled=True)  16.8 us
  transfers between devices with their start and end apart: 5, of which 4 were waited for; matrix products, arithmetic and copies ran while one was open for 32% of the time, Pallas kernels for 0%

profile of v1, /device:TPU:1, one launch (start us, length us, event | category | flops | bytes accessed | tf_op | source)
XLA Modules:
  0.0 802.1 jit_solution(10875709716127795163)
XLA Ops:
  7.5 1.9 fusion.53
  9.5 359.1 %all-reduce.4.cloned.1.call-done = f32[768,768]{0,1:T(8,128)} async-done(((f32[768,768]{0,1:T(8,128)}), f32[768,768]{0,1:T(8,128)}) %all-reduce.4.cloned.1.call-update) | async-done | bytes 2359312 | tf_op jit(solution)/shard_map/psum | solution.py:47
  369.3 1.4 scatter_custom_fusion
  371.5 13.6 %all-to-all-start = ((s32[128,4,1]{1,2,0:T(1,128)}), s32[128,4,1]{1,2,0:T(1,128)S(1)}, u32[]{:S(2)}, u32[]{:S(2)}) async-start(s32[128,4,1]{1,2,0:T(1,128)} %bitcast.4), calls=%async_computation | async-start | bytes 131072 | tf_op jit(solution)/shard_map/all_to_all | solution.py:68
  386.1 1.6 fusion.11
  387.6 59.8 %all-reduce.6.cloned.1.call-done = f32[768,768]{0,1:T(8,128)} async-done(((f32[768,768]{0,1:T(8,128)}), f32[768,768]{0,1:T(8,128)}) %all-reduce.6.cloned.1.call-update) | async-done | bytes 2359312 | tf_op jit(solution)/shard_map/psum | solution.py:47
  447.5 3.3 select_add_fusion
  450.8 3.7 copy.39
  454.5 2.0 fusion
  457.9 11.7 %cholesky.164 = f32[128,128]{1,0:T(8,128)S(1)} custom-call(f32[128,128]{1,0:T(8,128)S(1)} %cholesky.421), custom_call_target="Cholesky" | custom-call | tf_op jit(solution)/shard_map/jit(cholesky)/cholesky | solution.py:48
  469.6 9.8 %custom-call.47 = f32[1,128,128]{1,2,0:T(8,128)S(1)} custom-call(f32[1,128,128]{2,1,0:T(8,128)S(1)} %get-tuple-element.46), custom_call_target="InvertDiagBlocksLowerTriangular" | custom-call | tf_op jit(solution)/shard_map/jit(cholesky)/cholesky | solution.py:48
  479.4 1.4 fusion.33
  480.8 1.4 convolution_subtract_fusion.4
  482.3 11.7 %cholesky.187 = f32[128,128]{1,0:T(8,128)S(1)} custom-call(f32[128,128]{1,0:T(8,128)S(1)} %cholesky.425), custom_call_target="Cholesky" | custom-call | tf_op jit(solution)/shard_map/jit(cholesky)/cholesky | solution.py:48
  495.0 10.6 %custom-call.48 = f32[1,128,128]{1,2,0:T(8,128)} custom-call(f32[1,128,128]{2,1,0:T(8,128)S(1)} %get-tuple-element.44), custom_call_target="InvertDiagBlocksLowerTriangular" | custom-call | tf_op jit(solution)/shard_map/jit(cholesky)/cholesky | solution.py:48
  507.1 1.9 convolution_subtract_fusion.5
  509.0 11.7 %cholesky.352 = f32[128,128]{1,0:T(8,128)S(1)} custom-call(f32[128,128]{1,0:T(8,128)S(1)} %cholesky.430), custom_call_target="Cholesky" | custom-call | tf_op jit(solution)/shard_map/jit(cholesky)/cholesky | solution.py:48
  520.9 9.8 %custom-call.49 = f32[1,128,128]{1,2,0:T(8,128)S(1)} custom-call(f32[1,128,128]{2,1,0:T(8,128)S(1)} %get-tuple-element.42), custom_call_target="InvertDiagBlocksLowerTriangular" | custom-call | tf_op jit(solution)/shard_map/jit(cholesky)/cholesky | solution.py:48
  531.1 2.1 convolution_subtract_fusion.6
  533.2 12.1 %cholesky.371 = f32[128,128]{1,0:T(8,128)S(1)} custom-call(f32[128,128]{1,0:T(8,128)S(1)} %cholesky.435), custom_call_target="Cholesky" | custom-call | tf_op jit(solution)/shard_map/jit(cholesky)/cholesky | solution.py:48
  545.5 9.8 %custom-call.50 = f32[1,128,128]{1,2,0:T(8,128)S(1)} custom-call(f32[1,128,128]{2,1,0:T(8,128)S(1)} %get-tuple-element.40), custom_call_target="InvertDiagBlocksLowerTriangular" | custom-call | tf_op jit(solution)/shard_map/jit(cholesky)/cholesky | solution.py:48
  555.6 1.9 convolution_subtract_fusion.7
  557.5 11.7 %cholesky.390 = f32[128,128]{1,0:T(8,128)S(1)} custom-call(f32[128,128]{1,0:T(8,128)S(1)} %cholesky.440), custom_call_target="Cholesky" | custom-call | tf_op jit(solution)/shard_map/jit(cholesky)/cholesky | solution.py:48
  569.4 9.8 %custom-call.51 = f32[1,128,128]{1,2,0:T(8,128)S(1)} custom-call(f32[1,128,128]{2,1,0:T(8,128)S(1)} %get-tuple-element.38), custom_call_target="InvertDiagBlocksLowerTriangular" | custom-call | tf_op jit(solution)/shard_map/jit(cholesky)/cholesky | solution.py:48
  579.5 1.7 convolution_subtract_fusion.8
  581.2 11.7 %cholesky.408 = f32[128,128]{1,0:T(8,128)S(1)} custom-call(f32[128,128]{1,0:T(8,128)S(1)} %convolution_subtract_fusion.8), custom_call_target="Cholesky" | custom-call | tf_op jit(solution)/shard_map/jit(cholesky)/cholesky | solution.py:48
  600.1 1.6 select_select_fusion
  601.6 21.3 %while.1 = (s32[]{:T(128)}, f32[768,768]{0,1:T(8,128)}, s32[6,2]{0,1:T(2,128)S(1)}, f32[6,128,128]{2,1,0:T(8,128)}, s32[]{:T(128)}) while((s32[]{:T(128)}, f32[768,768]{0,1:T(8,128)}, s32[6,2]{0,1:T(2,128)S(1)}, f32[6,128,128]{2,1,0:T(8,128)}, s32[]{:T(128)}) %tuple.34), condition=%wide.while_cond, body=%wide.while_body.sunk | while | flops 2 | bytes 393829 | solution.py:49
  602.3 2.2 dynamic-slice.7
  605.8 2.2 dynamic-slice.7
  609.4 2.2 dynamic-slice.7
  613.0 2.2 dynamic-slice.7
  616.5 2.2 dynamic-slice.7
  620.1 2.1 dynamic-slice.7
  622.9 59.9 %custom-call.52 = f32[6,128,128]{1,2,0:T(8,128)S(1)} custom-call(f32[6,128,128]{2,1,0:T(8,128)} %get-tuple-element.12), custom_call_target="InvertDiagBlocksLowerTriangular" | custom-call | tf_op jit(solution)/shard_map/jit(_solve_triangular)/triangular_solve | solution.py:49
  684.1 1.8 convolution_subtract_fusion.2
  686.4 2.3 convolution_subtract_fusion.3
  689.3 3.0 convolution_subtract_fusion.1
  693.0 3.6 fusion.12
  697.2 4.6 convolution_subtract_fusion
  702.7 1.5 scatter_custom_fusion.1
  705.0 16.8 %all-to-all-start.1 = ((bf16[128,4,192]{2,1,0:T(4,128)(2,1)}), bf16[128,4,192]{2,1,0:T(4,128)(2,1)S(1)}, u32[]{:S(2)}, u32[]{:S(2)}) async-start(bf16[128,4,192]{2,1,0:T(4,128)(2,1)} %all_to_all.27), calls=%async_computation.1 | async-start | bytes 524288 | tf_op jit(solution)/shard_map/all_to_all | solution.py:67
  723.4 20.9 %all-to-all-done.1 = bf16[128,4,192]{2,1,0:T(4,128)(2,1)S(1)} async-done(((bf16[128,4,192]{2,1,0:T(4,128)(2,1)}), bf16[128,4,192]{2,1,0:T(4,128)(2,1)S(1)}, u32[]{:S(2)}, u32[]{:S(2)}) %all-to-all-start.1) | async-done | bytes 196640 | tf_op jit(solution)/shard_map/all_to_all | solution.py:67
  744.5 11.7 %all_gather.6 = bf16[512,768]{0,1:T(8,128)(2,1)S(1)} all-gather(bf16[512,192]{0,1:T(8,128)(2,1)S(1)} %copy.58), channel_id=1, replica_groups=mesh['dp'=128,'mp'=4] {'mp'}, dimensions={1}, use_global_device_ids=true | all-gather | bytes 983040 | tf_op jit(solution)/shard_map/all_gather | solution.py:70
  757.0 5.2 all-gather
  764.2 12.3 %all-to-all-start.2 = ((f32[128,4,1]{1,2,0:T(1,128)}), f32[128,4,1]{1,2,0:T(1,128)S(1)}, u32[]{:S(2)}, u32[]{:S(2)}) async-start(f32[128,4,1]{1,2,0:T(1,128)} %bitcast.24), calls=%async_computation.2 | async-start | bytes 131072 | tf_op jit(solution)/shard_map/all_to_all | solution.py:77
  776.5 15.1 %all-to-all-done.2 = f32[128,4,1]{1,2,0:T(1,128)S(1)} async-done(((f32[128,4,1]{1,2,0:T(1,128)}), f32[128,4,1]{1,2,0:T(1,128)S(1)}, u32[]{:S(2)}, u32[]{:S(2)}) %all-to-all-start.2) | async-done | bytes 2080 | tf_op jit(solution)/shard_map/all_to_all | solution.py:77
  792.5 2.5 gather_fusion
  (123 shorter events, 30.9 us)
Async XLA Ops:
  6.5 1.0 copy-start
  6.5 362.1 %all-reduce.4.cloned.1.call-start = ((), (), s32[]{:S(2)}) async-start(), calls=%async_computation.3 | async-start | bytes 4718592 | tf_op jit(solution)/shard_map/psum | solution.py:47
  9.5 359.2 %copy-start.5 = (s32[256]{0:T(256)S(1)}, s32[256]{0:T(256)}, u32[]{:S(2)}) copy-start(s32[256]{0:T(256)} %param.3) | copy-start | bytes 3076
  9.5 438.0 %all-reduce.6.cloned.1.call-start = ((), (), s32[]{:S(2)}) async-start(), calls=%async_computation.4 | async-start | bytes 4718592 | tf_op jit(solution)/shard_map/psum | solution.py:47
  371.5 333.6 %all-to-all-start = ((s32[128,4,1]{1,2,0:T(1,128)}), s32[128,4,1]{1,2,0:T(1,128)S(1)}, u32[]{:S(2)}, u32[]{:S(2)}) async-start(s32[128,4,1]{1,2,0:T(1,128)} %bitcast.4), calls=%async_computation | async-start | bytes 131072 | tf_op jit(solution)/shard_map/all_to_all | solution.py:68
  450.8 3.7 copy-start.1
  456.5 1.4 copy-start.3
  505.6 1.1 copy-start.4
  622.9 63.5 %copy-start.2 = (f32[768,768]{0,1:T(8,128)S(1)}, f32[768,768]{0,1:T(8,128)}, u32[]{:S(2)}) copy-start(f32[768,768]{0,1:T(8,128)} %fusion.11) | copy-start | bytes 7077892
  705.0 39.2 %all-to-all-start.1 = ((bf16[128,4,192]{2,1,0:T(4,128)(2,1)}), bf16[128,4,192]{2,1,0:T(4,128)(2,1)S(1)}, u32[]{:S(2)}, u32[]{:S(2)}) async-start(bf16[128,4,192]{2,1,0:T(4,128)(2,1)} %all_to_all.27), calls=%async_computation.1 | async-start | bytes 524288 | tf_op jit(solution)/shard_map/all_to_all | solution.py:67
  764.2 27.4 %all-to-all-start.2 = ((f32[128,4,1]{1,2,0:T(1,128)}), f32[128,4,1]{1,2,0:T(1,128)S(1)}, u32[]{:S(2)}, u32[]{:S(2)}) async-start(f32[128,4,1]{1,2,0:T(1,128)} %bitcast.24), calls=%async_computation.2 | async-start | bytes 131072 | tf_op jit(solution)/shard_map/all_to_all | solution.py:77
Sparse Core Ops, SparseCore 0:
  10.7 357.8 all-reduce.3
  371.0 76.4 all-reduce.5
